TPU v7x, 256 devices: a whole 4x4x8 slice. The times are simulated.
256 devices in a mesh: dp: 8 (over x, core), grid: 32 (over y, z).
Axes of the slice: x: 4, y: 4, z: 8, core: 2. Of those that a mesh axis runs over, the one named last changes fastest.
Arguments:
- q_row: bfloat16 [16, 96, 96, 1536], P('dp', 'grid'), may hold values from -8 to 8, as said below
- k_row: bfloat16 [16, 96, 96, 1536], P('dp', 'grid'), may hold values from -8 to 8
- v_row: bfloat16 [16, 96, 96, 1536], P('dp', 'grid'), may hold values from -6 to 6
- q_col: bfloat16 [16, 96, 96, 1536], P('dp', None, 'grid'), may hold values from -8 to 8, as said below
- k_col: bfloat16 [16, 96, 96, 1536], P('dp', None, 'grid'), may hold values from -8 to 8
- cotangent: bfloat16 [16, 96, 96, 1536], P('dp', None, 'grid'), may hold values from -6 to 6
- w_value: bfloat16 [1536, 1536], P(('dp', 'grid')), may hold values from -0.15625 to 0.15625
- row_positions: int32 [96], replicated, may hold values from 0 to 95, each once
- col_positions: int32 [96], replicated, may hold values from 0 to 95, each once
- mlp_in: float32 [512], P('grid'), may hold values from -8 to 8
- mlp_bias: float32 [512], P('grid'), may hold values from -4 to 4
- mlp_out: float32 [512, 48], P('grid'), may hold values from -0.08 to 0.08
Outputs:
- attended: bfloat16 [16, 96, 96, 1536], P('dp', None, 'grid')
- grad_mlp_in: float32 [512], P('grid')
- grad_mlp_bias: float32 [512], P('grid')
- grad_mlp_out: float32 [512, 48], P('grid')
Inputs may be any that keep to these rules, and one draw needn't show every extreme that they name: q_row and k_row lie within the range. q_col and k_col lie within the range. `row_positions`: each of 0 to 95 appears once. `col_positions`: each of 0 to 95 appears once.
All inputs are finite; a program needn't handle non-finite values.
Results may differ from a plain program's by a relative error of at most 0.007.
Values may be sent and summed in bfloat16 or wider, within the bound.
No kernel may reach another device: no remote copies, remote signals or barrier semaphores. Data moves between devices by JAX's collectives and lax.ppermute only.
A program may use at most 192 MiB of HBM per device.

v0:
```python
import jax
import jax.numpy as jnp
from jax import lax
from jax.sharding import PartitionSpec as P

G = 96
D = 1536
NH = 48
HD = 32
NOFF = 191
PRECISE = lax.Precision.HIGHEST


def offset_coords():
    delta = jnp.arange(NOFF, dtype=jnp.float32) - (G - 1)
    scaled = delta * (8.0 / (G - 1))
    return jnp.sign(scaled) * jnp.log2(jnp.abs(scaled) + 1.0) / 3.0


def offset_one_hot(positions):
    spread = positions[:, None] - positions[None, :] + (G - 1)
    levels = jnp.arange(NOFF, dtype=jnp.int32)
    return (spread.reshape(-1)[:, None] == levels[None, :]).astype(jnp.float32)


def expand_bias(one_hot, bias_table):
    flat_bias = jnp.dot(one_hot, bias_table, precision=PRECISE)
    return flat_bias.reshape(G, G, NH).transpose(2, 0, 1)


def fold_bias(one_hot, bias_grad):
    flat_grad = bias_grad.transpose(1, 2, 0).reshape(G * G, NH)
    return lax.dot_general(one_hot, flat_grad, (((0,), (0,)), ((), ())), precision=PRECISE)


def soft_grad(attn_probs, d_probs):
    return attn_probs * (d_probs - jnp.sum(attn_probs * d_probs, axis=-1, keepdims=True))


def fetch_weight(w_value):
    return lax.all_gather(w_value, ("dp", "grid"), axis=0, tiled=True)


def shards(
    q_row,
    k_row,
    v_row,
    q_col,
    k_col,
    cotangent,
    w_value,
    row_positions,
    col_positions,
    mlp_in,
    mlp_bias,
    mlp_out,
):
    images = q_row.shape[0]
    row_count = q_row.shape[1]
    col_count = q_col.shape[2]
    coords = offset_coords()
    pre_act = coords[:, None] * mlp_in[None, :] + mlp_bias[None, :]
    hidden_units = jnp.maximum(pre_act, 0.0)
    partial_table = jnp.dot(hidden_units, mlp_out, precision=PRECISE)
    table_pre = lax.psum(partial_table, "grid")
    squashed = jax.nn.sigmoid(table_pre)
    bias_table = 16.0 * squashed
    hot_cols = offset_one_hot(col_positions)
    hot_rows = offset_one_hot(row_positions)
    bias_row = expand_bias(hot_cols, bias_table)
    bias_col = expand_bias(hot_rows, bias_table)
    score_scale = HD ** (-0.5)
    query_rows = q_row.reshape(images * row_count, G, NH, HD)
    key_rows = k_row.reshape(images * row_count, G, NH, HD)
    value_rows = v_row.reshape(images * row_count, G, NH, HD)
    scores = (
        jnp.einsum("nqhd,nkhd->nhqk", query_rows, key_rows, preferred_element_type=jnp.float32)
        * score_scale
        + bias_row[None]
    )
    p_row = jax.nn.softmax(scores, axis=-1)
    p_row_b = p_row.astype(jnp.bfloat16)
    row_out = jnp.einsum(
        "nhqk,nkhd->nqhd", p_row_b, value_rows, preferred_element_type=jnp.float32
    ).astype(jnp.bfloat16)
    flat_out = row_out.reshape(images * row_count * G, D)
    whole_weight = fetch_weight(w_value)
    projected = jnp.dot(flat_out, whole_weight, preferred_element_type=jnp.float32)
    values = projected.astype(jnp.bfloat16).reshape(images, row_count, G, D)
    col_values = lax.all_to_all(values, "grid", split_axis=2, concat_axis=1, tiled=True)
    query_cols = q_col.reshape(images, G, col_count, NH, HD)
    key_cols = k_col.reshape(images, G, col_count, NH, HD)
    value_cols = col_values.reshape(images, G, col_count, NH, HD)
    scores_col = (
        jnp.einsum("bqchd,bkchd->bchqk", query_cols, key_cols, preferred_element_type=jnp.float32)
        * score_scale
        + bias_col
    )
    p_col = jax.nn.softmax(scores_col, axis=-1)
    p_col_b = p_col.astype(jnp.bfloat16)
    attended = (
        jnp.einsum("bchqk,bkchd->bqchd", p_col_b, value_cols, preferred_element_type=jnp.float32)
        .astype(jnp.bfloat16)
        .reshape(images, G, col_count, D)
    )
    grad_cols = cotangent.reshape(images, G, col_count, NH, HD)
    dprob_col = jnp.einsum(
        "bqchd,bkchd->bchqk", grad_cols, value_cols, preferred_element_type=jnp.float32
    )
    ds_col = soft_grad(p_col, dprob_col)
    col_table = fold_bias(hot_rows, jnp.sum(ds_col, axis=(0, 1)))
    col_summed = lax.psum(col_table, ("dp", "grid"))
    d_values = (
        jnp.einsum("bchqk,bqchd->bkchd", p_col_b, grad_cols, preferred_element_type=jnp.float32)
        .astype(jnp.bfloat16)
        .reshape(images, G, col_count, D)
    )
    d_rows = lax.all_to_all(d_values, "grid", split_axis=1, concat_axis=2, tiled=True)
    flat_grad = d_rows.reshape(images * row_count * G, D)
    d_flat = lax.dot_general(
        flat_grad, whole_weight, (((1,), (1,)), ((), ())), preferred_element_type=jnp.float32
    )
    d_row_out = d_flat.astype(jnp.bfloat16).reshape(images * row_count, G, NH, HD)
    dprob_row = jnp.einsum(
        "nqhd,nkhd->nhqk", d_row_out, value_rows, preferred_element_type=jnp.float32
    )
    ds_row = soft_grad(p_row, dprob_row)
    row_table = fold_bias(hot_cols, jnp.sum(ds_row, axis=0))
    table_sum = col_summed + lax.psum(row_table, ("dp", "grid"))
    batch_size = lax.axis_size("dp") * images
    table_grad = table_sum / (batch_size * G)
    pre_grad = table_grad * 16.0 * squashed * (1.0 - squashed)
    grad_mlp_out = lax.dot_general(
        hidden_units, pre_grad, (((0,), (0,)), ((), ())), precision=PRECISE
    )
    back_units = lax.dot_general(pre_grad, mlp_out, (((1,), (1,)), ((), ())), precision=PRECISE)
    unit_grad = jnp.where(pre_act > 0, back_units, 0.0)
    grad_mlp_in = jnp.sum(unit_grad * coords[:, None], axis=0)
    grad_mlp_bias = jnp.sum(unit_grad, axis=0)
    return (attended, grad_mlp_in, grad_mlp_bias, grad_mlp_out)


def solution(mesh):
    return jax.shard_map(
        shards,
        mesh=mesh,
        in_specs=(
            P("dp", "grid", None, None),
            P("dp", "grid", None, None),
            P("dp", "grid", None, None),
            P("dp", None, "grid", None),
            P("dp", None, "grid", None),
            P("dp", None, "grid", None),
            P(("dp", "grid"), None),
            P(),
            P(),
            P("grid"),
            P("grid"),
            P("grid", None),
        ),
        out_specs=(P("dp", None, "grid", None), P("grid"), P("grid"), P("grid", None)),
        check_vma=False,
    )
```

profile of v0, /device:TPU:1, one launch (start us, length us, event | category | flops | bytes accessed | tf_op | source)
XLA Modules:
  0.0 479.7 jit_solution(3552161299242555741)
XLA Ops:
  10.4 119.0 %psum.21 = f32[191,48]{0,1:T(8,128)S(1)} all-reduce(f32[191,48]{0,1:T(8,128)S(1)} %fusion.55), channel_id=1, replica_groups=mesh['dp'=8,'grid'=32] {'grid'}, use_global_device_ids=true, to_apply=%region_0.0 | all-reduce | flops 9168 | bytes 73344 | tf_op jit(solution)/shard_map/psum | solution.py:65
  129.4 4.4 fusion.11
  138.0 4.1 copy.132
  144.6 2.9 copy.137
  147.5 11.3 %fusion.79 = (f32[2,3,48,96]{3,2,1,0:T(8,128)S(1)}, f32[2,3,48,96,96]{3,4,2,1,0:T(8,128)}) fusion(f32[48,96,96]{1,2,0:T(8,128)} %bitcast.78, bf16[2,96,3,48,32]{1,4,3,2,0:T(8,128)(2,1)} %bitcast.86, bf16[2,96,3,48,32]{1,4,3,2,0:T(8,128)(2,1)} %bitcast.87), kind=kOutput, calls=%fused_computation.87 | convolution fusion | flops 180486240 | bytes 16035840 | tf_op jit(solution)/shard_map/sub | solution.py:99
  158.8 10.2 %fusion.35 = bf16[2,3,48,96,32]{3,4,2,1,0:T(8,128)(2,1)} fusion(bf16[2,96,3,48,32]{1,4,3,2,0:T(8,128)(2,1)S(1)} %bitcast.75, f32[2,3,48,96,96]{3,4,2,1,0:T(8,128)} %get-tuple-element.33, f32[2,3,48,96]{3,2,1,0:T(8,128)S(1)} %get-tuple-element.32), kind=kOutput, calls=%fused_computation.47 | convolution fusion | flops 176062464 | bytes 14266368 | tf_op jit(solution)/shard_map/bchqk,bqchd->bkchd/dot_general | solution.py:114
  169.1 5.3 %copy.141 = bf16[2,96,3,1536]{3,0,2,1:T(2,128)(2,1)} copy(bf16[2,96,3,1536]{1,3,2,0:T(8,128)(2,1)} %bitcast.90) | data formatting | bytes 3538944 | tf_op jit(solution)/shard_map/reshape | solution.py:116
  174.4 5.0 %all-to-all-start.1 = ((bf16[2,96,3,1536]{3,0,2,1:T(2,128)(2,1)}), bf16[2,96,3,1536]{3,0,2,1:T(2,128)(2,1)}, u32[]{:S(2)}, u32[]{:S(2)}) async-start(bf16[2,96,3,1536]{3,0,2,1:T(2,128)(2,1)} %copy.141), calls=%async_computation.1 | async-start | bytes 3538944 | tf_op jit(solution)/shard_map/all_to_all | solution.py:118
  179.6 4.5 fusion.17
  188.2 4.1 copy.123
  194.8 4.2 copy.126
  198.9 11.3 %fusion.78 = (f32[6,48,96]{2,1,0:T(8,128)S(1)}, f32[6,48,96,96]{2,3,1,0:T(8,128)}) fusion(f32[48,96,96]{1,2,0:T(8,128)S(1)} %bitcast.79, bf16[6,96,48,32]{1,3,2,0:T(8,128)(2,1)} %bitcast.88, bf16[6,96,48,32]{1,3,2,0:T(8,128)(2,1)} %bitcast.89), kind=kOutput, calls=%fused_computation.86 | convolution fusion | flops 180486240 | bytes 16035840 | tf_op jit(solution)/shard_map/sub | solution.py:81
  210.2 7.7 %convert_bitcast_fusion = bf16[6,96,48,32]{1,3,2,0:T(8,128)(2,1)S(1)} fusion(bf16[6,96,48,32]{1,3,2,0:T(8,128)(2,1)} %bitcast.82, f32[6,48,96,96]{2,3,1,0:T(8,128)} %get-tuple-element.31, f32[6,48,96]{2,1,0:T(8,128)S(1)} %get-tuple-element.30), kind=kOutput, calls=%fused_computation.44 | convolution fusion | flops 176062464 | bytes 14266368 | tf_op jit(solution)/shard_map/nhqk,nkhd->nqhd/dot_general | solution.py:83
  218.0 2.8 copy.128
  220.8 3.1 reshape.125
  226.3 3.2 reshape.135
  229.5 8.5 %reshape.139 = bf16[1536,1536]{1,0:T(8,128)(2,1)} reshape(bf16[256,6,1536]{2,1,0:T(8,128)(2,1)} %all-gather.3.cloned.1.call-done) | data formatting | bytes 9437184
  238.0 6.4 %convolution_convert_fusion.1 = bf16[576,1536]{1,0:T(8,128)(2,1)} fusion(bf16[576,1536]{1,0:T(8,128)(2,1)S(1)} %copy-done.9, bf16[1536,1536]{1,0:T(8,128)(2,1)} %reshape.139), kind=kOutput, calls=%fused_computation.41 | convolution fusion | flops 2718793728 | bytes 8257536 | tf_op jit(solution)/shard_map/dot_general | solution.py:120
  247.1 3.6 reshape.136
  250.8 5.9 %convolution_convert_fusion = bf16[576,1536]{1,0:T(8,128)(2,1)S(1)} fusion(bf16[576,1536]{0,1:T(8,128)(2,1)} %reshape.125, bf16[1536,1536]{1,0:T(8,128)(2,1)} %reshape.139), kind=kOutput, calls=%fused_computation.40 | convolution fusion | flops 2718793728 | bytes 8257536 | tf_op jit(solution)/shard_map/dot_general | solution.py:88
  256.6 3.0 copy.129
  259.7 10.2 %all-to-all-start = ((bf16[2,3,96,1536]{3,0,1,2:T(2,128)(2,1)}), bf16[2,3,96,1536]{3,0,1,2:T(2,128)(2,1)}, u32[]{:S(2)}, u32[]{:S(2)}) async-start(bf16[2,3,96,1536]{3,0,1,2:T(2,128)(2,1)} %copy.129), calls=%async_computation | async-start | bytes 3538944 | tf_op jit(solution)/shard_map/all_to_all | solution.py:90
  269.9 10.4 %fusion = f32[6,48,96,96]{2,3,1,0:T(8,128)} fusion(bf16[6,96,48,32]{1,3,2,0:T(8,128)(2,1)} %bitcast.83, bf16[6,96,48,32]{1,0,3,2:T(8,128)(2,1)S(1)} %copy-done.4, f32[6,48,96,96]{2,3,1,0:T(8,128)} %get-tuple-element.31, f32[6,48,96]{2,1,0:T(8,128)S(1)} %get-tuple-element.30), kind=kOutput, calls=%fused_computation | convolution fusion | flops 175205472 | bytes 24883200 | tf_op jit(solution)/shard_map/sub | solution.py:37
  280.3 13.5 %multiply_reduce_fusion = f32[48,96,96]{1,2,0:T(8,128)} fusion(f32[6,48,96,96]{2,3,1,0:T(8,128)} %fusion, f32[6,48,96,96]{2,3,1,0:T(8,128)} %get-tuple-element.31, f32[6,48,96]{2,1,0:T(8,128)S(1)} %get-tuple-element.30, bf16[6,96,48,32]{1,3,2,0:T(8,128)(2,1)} %bitcast.84, bf16[6,96,48,32]{1,0,3,2:T(8,128)(2,1)S(1)} %copy-done.4), kind=kOutput, calls=%fused_computation.8 | convolution fusion | flops 180043776 | bytes 26652672 | tf_op jit(solution)/shard_map/nqhd,nkhd->nhqk/dot_general | solution.py:124
  301.0 6.1 %reshape.127 = bf16[2,96,3,48,32]{4,3,0,2,1:T(8,128)(2,1)} reshape(bf16[2,32,3,3,1536]{4,0,3,2,1:T(2,128)(2,1)S(1)} %copy.131) | data formatting | bytes 3538944 | tf_op jit(solution)/shard_map/reshape | solution.py:93
  307.2 8.3 %copy.135 = bf16[2,96,3,48,32]{1,4,3,2,0:T(8,128)(2,1)} copy(bf16[2,96,3,48,32]{4,3,0,2,1:T(8,128)(2,1)} %reshape.127) | data formatting | bytes 3538944 | tf_op jit(solution)/shard_map/reshape | solution.py:93
  315.5 9.4 %fusion.32 = bf16[2,3,48,32,96]{4,3,2,1,0:T(8,128)(2,1)} fusion(bf16[2,96,3,48,32]{1,4,3,2,0:T(8,128)(2,1)} %copy.135, f32[2,3,48,96,96]{3,4,2,1,0:T(8,128)} %get-tuple-element.33, f32[2,3,48,96]{3,2,1,0:T(8,128)S(1)} %get-tuple-element.32), kind=kOutput, calls=%fused_computation.46 | convolution fusion | flops 176062464 | bytes 14266368 | tf_op jit(solution)/shard_map/bchqk,bkchd->bqchd/dot_general | solution.py:102
  325.0 6.3 %fusion.80 = f32[2,3,48,96,96]{4,3,2,1,0:T(8,128)} fusion(bf16[2,96,3,48,32]{1,4,3,2,0:T(8,128)(2,1)S(1)} %copy-done.3, bf16[2,96,3,48,32]{1,4,3,2,0:T(8,128)(2,1)S(1)} %bitcast.76), kind=kOutput, calls=%fused_computation.88 | convolution fusion | flops 169869312 | bytes 14155776 | tf_op jit(solution)/shard_map/bqchd,bkchd->bchqk/dot_general | solution.py:107
  331.2 17.8 %fusion.5 = f32[48,96,96]{1,2,0:T(8,128)} fusion(f32[2,3,48,96,96]{4,3,2,1,0:T(8,128)} %fusion.80, f32[2,3,48,96,96]{3,4,2,1,0:T(8,128)} %get-tuple-element.33, f32[2,3,48,96]{3,2,1,0:T(8,128)S(1)} %get-tuple-element.32, bf16[2,96,3,48,32]{1,4,3,2,0:T(8,128)(2,1)} %copy.135, bf16[2,96,3,48,32]{1,4,3,2,0:T(8,128)(2,1)S(1)} %bitcast.77), kind=kOutput, calls=%fused_computation.7 | convolution fusion | flops 185379936 | bytes 26652672 | tf_op jit(solution)/shard_map/sub | solution.py:37
  353.6 5.4 %fusion.10 = f32[191,48]{0,1:T(8,128)S(1)} fusion(f32[9216,48]{0,1:T(8,128)} %reshape.133, s32[9216]{0:T(1024)S(1)} %copy-done.11), kind=kOutput, calls=%fused_computation.20 | convolution fusion | flops 1015667712 | bytes 1843008 | tf_op jit(solution)/shard_map/dot_general | solution.py:33
  359.0 5.3 %fusion.46 = f32[191,48]{0,1:T(8,128)S(1)} fusion(f32[191,48]{0,1:T(8,128)S(1)} %fusion.10, f32[9216,48]{0,1:T(8,128)} %reshape.137, s32[9216]{0:T(1024)S(1)} %add.74), kind=kOutput, calls=%fused_computation.49 | convolution fusion | flops 1015676864 | bytes 1879680 | tf_op jit(solution)/shard_map/dot_general | solution.py:33
  364.3 104.5 %psum.24 = f32[191,48]{0,1:T(8,128)S(1)} all-reduce(f32[191,48]{0,1:T(8,128)S(1)} %fusion.46), channel_id=1, replica_groups=mesh['dp'=8,'grid'=32] {'dp','grid'}, use_global_device_ids=true, to_apply=%region_7.0 | all-reduce | flops 9168 | bytes 73344 | tf_op jit(solution)/shard_map/psum | solution.py:112
  (61 shorter events, 37.4 us)
Async XLA Ops:
  7.2 2.3 copy-start
  7.2 222.3 %all-gather.3.cloned.1.call-start = ((), (), s32[]{:S(2)}) async-start(), calls=%async_computation.2 | async-start | bytes 6316032 | tf_op jit(solution)/shard_map/all_gather | solution.py:41
  8.8 120.6 %copy-start.10 = (s32[9216]{0:T(1024)}, s32[9216]{0:T(1024)S(1)}, u32[]{:S(2)}) copy-start(s32[9216]{0:T(1024)S(1)} %add.83) | copy-start | bytes 110596
  8.9 0.6 copy-start.15
  138.0 4.1 copy-start.7
  147.5 11.3 %copy-start.1 = (bf16[2,96,3,1536]{1,3,2,0:T(8,128)(2,1)}, bf16[2,96,3,1536]{1,3,2,0:T(8,128)(2,1)S(1)}, u32[]{:S(2)}) copy-start(bf16[2,96,3,1536]{1,3,2,0:T(8,128)(2,1)S(1)} %copy.137) | copy-start | bytes 5308420
  174.3 5.0 %copy-start.12 = (s32[96]{0:T(128)S(1)}, s32[96]{0:T(128)}, u32[]{:S(2)}) copy-start(s32[96]{0:T(128)} %param.20) | copy-start | bytes 1156
  174.4 49.6 %all-to-all-start.1 = ((bf16[2,96,3,1536]{3,0,2,1:T(2,128)(2,1)}), bf16[2,96,3,1536]{3,0,2,1:T(2,128)(2,1)}, u32[]{:S(2)}, u32[]{:S(2)}) async-start(bf16[2,96,3,1536]{3,0,2,1:T(2,128)(2,1)} %copy.141), calls=%async_computation.1 | async-start | bytes 3538944 | tf_op jit(solution)/shard_map/all_to_all | solution.py:118
  188.2 4.1 copy-start.8
  194.8 4.2 copy-start.5
  229.5 8.5 %copy-start.9 = (bf16[576,1536]{1,0:T(8,128)(2,1)S(1)}, bf16[576,1536]{1,0:T(8,128)(2,1)}, u32[]{:S(2)}) copy-start(bf16[576,1536]{1,0:T(8,128)(2,1)} %reshape.135) | copy-start | bytes 5308420
  259.7 10.2 %copy-start.4 = (bf16[6,96,48,32]{1,0,3,2:T(8,128)(2,1)S(1)}, bf16[6,96,48,32]{1,0,3,2:T(8,128)(2,1)}, u32[]{:S(2)}) copy-start(bf16[6,96,48,32]{1,0,3,2:T(8,128)(2,1)} %reshape.136) | copy-start | bytes 5308420
  259.7 38.7 %all-to-all-start = ((bf16[2,3,96,1536]{3,0,1,2:T(2,128)(2,1)}), bf16[2,3,96,1536]{3,0,1,2:T(2,128)(2,1)}, u32[]{:S(2)}, u32[]{:S(2)}) async-start(bf16[2,3,96,1536]{3,0,1,2:T(2,128)(2,1)} %copy.129), calls=%async_computation | async-start | bytes 3538944 | tf_op jit(solution)/shard_map/all_to_all | solution.py:90
  315.5 9.4 %copy-start.2 = (bf16[2,96,3,1536]{1,3,2,0:T(8,128)(2,1)S(1)}, bf16[2,96,3,1536]{1,3,2,0:T(8,128)(2,1)}, u32[]{:S(2)}) copy-start(bf16[2,96,3,1536]{1,3,2,0:T(8,128)(2,1)} %copy-done.1) | copy-start | bytes 5308420
  315.5 9.4 %copy-start.3 = (bf16[2,96,3,48,32]{1,4,3,2,0:T(8,128)(2,1)S(1)}, bf16[2,96,3,48,32]{1,4,3,2,0:T(8,128)(2,1)}, u32[]{:S(2)}) copy-start(bf16[2,96,3,48,32]{1,4,3,2,0:T(8,128)(2,1)} %copy.135) | copy-start | bytes 5308420
  351.0 2.5 copy-start.11
  353.6 115.2 %copy-start.13 = (f32[16]{0:T(128)S(1)}, f32[16]{0:T(128)}, u32[]{:S(2)}) copy-start(f32[16]{0:T(128)} %param.22) | copy-start | bytes 196
  353.6 115.2 %copy-start.14 = (f32[16]{0:T(128)S(1)}, f32[16]{0:T(128)}, u32[]{:S(2)}) copy-start(f32[16]{0:T(128)} %param.21) | copy-start | bytes 196
  353.6 115.2 %copy-start.16 = (f32[191]{0:T(256)S(1)}, f32[191]{0:T(256)}, u32[]{:S(2)}) copy-start(f32[191]{0:T(256)} %copy-done.15) | copy-start | bytes 2296
  353.6 116.8 %copy-start.6 = (bf16[2,3,48,32,96]{4,3,2,1,0:T(8,128)(2,1)S(1)}, bf16[2,3,48,32,96]{4,3,2,1,0:T(8,128)(2,1)}, u32[]{:S(2)}) copy-start(bf16[2,3,48,32,96]{4,3,2,1,0:T(8,128)(2,1)} %fusion.32) | copy-start | bytes 5308420
Sparse Core Ops, SparseCore 0:
  11.8 121.0 all-gather.2
where the time goes:
time: 489 us; the launch traced here: 480 us
  blocking collectives  224 us (46%)
  matrix products  132 us (27%)
  local copies, waits for them, and re-layouts  92.6 us (19%)
  starting transfers between devices  15.2 us (3%)
  between operations  14.5 us (3%)
    psum x1, blocking collectives, shards(): table_pre = lax.psum(partial_table, 'grid')  119 us
    psum x1, blocking collectives, shards(): col_summed = lax.psum(col_table, ('dp', 'grid'))  104 us
    unnamed x42, local copies, waits for them, and re-layouts  31.6 us
    sub x2, matrix products, soft_grad(): d_probs - jnp.sum(attn_probs * d_probs, axis=-1, keepdims=True)  28.2 us
    reshape x2, local copies, waits for them, and re-layouts, shards(): value_cols = col_values.reshape(images, G, col_count, NH, HD)  14.5 us
    dot_general x1, matrix products, shards(): jnp.einsum('nqhd,nkhd->nhqk', d_row_out, value_rows, preferred_element_ty...  13.5 us
    sub x1, matrix products, shards(): p_col = jax.nn.softmax(scores_col, axis=-1)  11.3 us
    sub x1, matrix products, shards(): p_row = jax.nn.softmax(scores, axis=-1)  11.3 us
  transfers between devices with their start and end apart: 3, of which 0 were waited for; matrix products, arithmetic and copies ran while one was open for 26% of the time, Pallas kernels for 0%

commit v1 on v0

--- a/solution.py
+++ b/solution.py
@@ -109,7 +109,7 @@
     )
     ds_col = soft_grad(p_col, dprob_col)
     col_table = fold_bias(hot_rows, jnp.sum(ds_col, axis=(0, 1)))
-    col_summed = lax.psum(col_table, ("dp", "grid"))
+    col_summed = jnp.sum(lax.all_gather(col_table, ("dp", "grid")), axis=0)
     d_values = (
         jnp.einsum("bchqk,bqchd->bkchd", p_col_b, grad_cols, preferred_element_type=jnp.float32)
         .astype(jnp.bfloat16)

time: 489 us -> 531 us (1.086)
  blocking collectives: 224 us -> 260 us
  starting transfers between devices: 15.2 us -> 4.93 us
  local copies, waits for them, and re-layouts: 92.6 us -> 101 us
  other arithmetic: 0.9 us -> 6.3 us
    all_to_all x0 -> x1, blocking collectives: none -> 34.6 us  [shards(): lax.all_to_all(d_values, 'grid', split_axis=1, concat_axis=2, tiled=True)]
    reduce_sum x0 -> x1, other arithmetic: none -> 5.41 us  [shards(): col_summed = jnp.sum(lax.all_gather(col_table, ('dp', 'grid')), axis=0)]
    all_to_all x1, starting transfers between devices: 10.2 us -> 4.85 us  [shards(): lax.all_to_all(values, 'grid', split_axis=2, concat_axis=1, tiled=True)]
    unnamed x42 -> x36, local copies, waits for them, and re-layouts: 31.6 us -> 33.4 us
  transfers between devices with their start and end apart: 3 -> 3, of which waited for: 0 -> 0; matrix products, arithmetic and copies ran while one was open for 26% -> 30% of each run, Pallas kernels for 0% -> 0%
where the time goes in v1:
time: 531 us; the launch traced here: 523 us
  blocking collectives  260 us (49%)
  matrix products  135 us (25%)
  local copies, waits for them, and re-layouts  101 us (19%)
  between operations  14.5 us (3%)
  other arithmetic  6.3 us (1%)
    psum x1, blocking collectives, shards(): table_pre = lax.psum(partial_table, 'grid')  119 us
    psum x1, blocking collectives, shards(): table_sum = col_summed + lax.psum(row_table, ('dp', 'grid'))  106 us
    all_to_all x1, blocking collectives, shards(): lax.all_to_all(d_values, 'grid', split_axis=1, concat_axis=2, tiled=True)  34.6 us
    unnamed x36, local copies, waits for them, and re-layouts  33.4 us
    sub x2, matrix products, soft_grad(): d_probs - jnp.sum(attn_probs * d_probs, axis=-1, keepdims=True)  29.7 us
    reshape x2, local copies, waits for them, and re-layouts, shards(): value_cols = col_values.reshape(images, G, col_count, NH, HD)  18.1 us
    dot_general x1, matrix products, shards(): jnp.einsum('nqhd,nkhd->nhqk', d_row_out, value_rows, preferred_element_ty...  13.7 us
    sub x1, matrix products, shards(): p_row = jax.nn.softmax(scores, axis=-1)  11.2 us
  transfers between devices with their start and end apart: 3, of which 0 were waited for; matrix products, arithmetic and copies ran while one was open for 30% of the time, Pallas kernels for 0%

profile of v1, /device:TPU:1, one launch (start us, length us, event | category | flops | bytes accessed | tf_op | source)
XLA Modules:
  0.0 523.0 jit_solution(225418333323062170)
XLA Ops:
  10.4 119.0 %psum.14 = f32[191,48]{0,1:T(8,128)S(1)} all-reduce(f32[191,48]{0,1:T(8,128)S(1)} %fusion.55), channel_id=1, replica_groups=mesh['dp'=8,'grid'=32] {'grid'}, use_global_device_ids=true, to_apply=%region_0.0 | all-reduce | flops 9168 | bytes 73344 | tf_op jit(solution)/shard_map/psum | solution.py:65
  129.4 4.4 fusion.17
  138.1 4.1 copy.123
  144.6 4.1 copy.126
  148.8 11.2 %fusion.74 = (f32[6,48,96]{2,1,0:T(8,128)S(1)}, f32[6,48,96,96]{2,3,1,0:T(8,128)}) fusion(f32[48,96,96]{1,2,0:T(8,128)S(1)} %bitcast.81, bf16[6,96,48,32]{1,3,2,0:T(8,128)(2,1)} %bitcast.88, bf16[6,96,48,32]{1,3,2,0:T(8,128)(2,1)} %bitcast.89), kind=kOutput, calls=%fused_computation.82 | convolution fusion | flops 180486240 | bytes 16035840 | tf_op jit(solution)/shard_map/sub | solution.py:81
  160.0 7.7 %convert_bitcast_fusion = bf16[6,96,48,32]{1,3,2,0:T(8,128)(2,1)S(1)} fusion(bf16[6,96,48,32]{1,3,2,0:T(8,128)(2,1)} %bitcast.85, f32[6,48,96,96]{2,3,1,0:T(8,128)} %get-tuple-element.31, f32[6,48,96]{2,1,0:T(8,128)S(1)} %get-tuple-element.30), kind=kOutput, calls=%fused_computation.44 | convolution fusion | flops 176062464 | bytes 14266368 | tf_op jit(solution)/shard_map/nhqk,nkhd->nqhd/dot_general | solution.py:83
  173.7 8.5 %reshape.140 = bf16[1536,1536]{1,0:T(8,128)(2,1)} reshape(bf16[256,6,1536]{2,1,0:T(8,128)(2,1)} %all-gather.6.cloned.1.call-done) | data formatting | bytes 9437184
  182.3 5.3 %convolution_convert_fusion = bf16[576,1536]{1,0:T(8,128)(2,1)S(1)} fusion(bf16[576,1536]{0,1:T(8,128)(2,1)S(1)} %copy-done.4, bf16[1536,1536]{1,0:T(8,128)(2,1)} %reshape.140), kind=kOutput, calls=%fused_computation.40 | convolution fusion | flops 2718793728 | bytes 8257536 | tf_op jit(solution)/shard_map/dot_general | solution.py:88
  190.6 4.8 all-to-all-start
  195.7 4.5 fusion.11
  204.7 4.1 copy.132
  214.2 10.6 %fusion.75 = (f32[2,3,48,96]{3,2,1,0:T(8,128)S(1)}, f32[2,3,48,96,96]{3,4,2,1,0:T(8,128)}) fusion(f32[48,96,96]{1,2,0:T(8,128)} %bitcast.82, bf16[2,96,3,48,32]{1,4,3,2,0:T(8,128)(2,1)} %bitcast.90, bf16[2,96,3,48,32]{1,4,3,2,0:T(8,128)(2,1)} %bitcast.91), kind=kOutput, calls=%fused_computation.83 | convolution fusion | flops 180486240 | bytes 16035840 | tf_op jit(solution)/shard_map/sub | solution.py:99
  224.7 3.9 copy.131
  228.6 9.8 %reshape.127 = bf16[2,96,3,48,32]{4,3,0,2,1:T(8,128)(2,1)} reshape(bf16[2,32,3,3,1536]{4,0,3,2,1:T(2,128)(2,1)} %copy.131) | data formatting | bytes 3538944 | tf_op jit(solution)/shard_map/reshape | solution.py:93
  238.4 8.4 %copy.135 = bf16[2,96,3,48,32]{1,4,3,2,0:T(8,128)(2,1)} copy(bf16[2,96,3,48,32]{4,3,0,2,1:T(8,128)(2,1)} %reshape.127) | data formatting | bytes 3538944 | tf_op jit(solution)/shard_map/reshape | solution.py:93
  246.8 8.7 %fusion.76 = f32[2,3,48,96,96]{4,3,2,1,0:T(8,128)} fusion(bf16[2,96,3,48,32]{1,4,3,2,0:T(8,128)(2,1)} %copy.135, bf16[2,96,3,48,32]{1,4,3,2,0:T(8,128)(2,1)S(1)} %bitcast.77), kind=kOutput, calls=%fused_computation.84 | convolution fusion | flops 169869312 | bytes 14155776 | tf_op jit(solution)/shard_map/bqchd,bkchd->bchqk/dot_general | solution.py:107
  255.4 18.1 %fusion.5 = f32[48,96,96]{1,2,0:T(8,128)} fusion(f32[2,3,48,96,96]{4,3,2,1,0:T(8,128)} %fusion.76, f32[2,3,48,96,96]{3,4,2,1,0:T(8,128)} %get-tuple-element.33, f32[2,3,48,96]{3,2,1,0:T(8,128)S(1)} %get-tuple-element.32, bf16[2,96,3,48,32]{1,4,3,2,0:T(8,128)(2,1)} %copy.135, bf16[2,96,3,48,32]{1,4,3,2,0:T(8,128)(2,1)S(1)} %bitcast.78), kind=kOutput, calls=%fused_computation.7 | convolution fusion | flops 185379936 | bytes 26652672 | tf_op jit(solution)/shard_map/sub | solution.py:37
  276.6 3.6 reshape.133
  280.2 5.9 %fusion.46 = f32[1,191,48]{1,2,0:T(8,128)} fusion(f32[9216,48]{0,1:T(8,128)} %reshape.133, s32[9216]{0:T(1024)S(1)} %add.81), kind=kOutput, calls=%fused_computation.49 | convolution fusion | flops 1015667712 | bytes 1843008 | tf_op jit(solution)/shard_map/dot_general | solution.py:33
  286.1 10.4 %fusion.35 = bf16[2,3,48,96,32]{3,4,2,1,0:T(8,128)(2,1)} fusion(bf16[2,96,3,48,32]{1,4,3,2,0:T(8,128)(2,1)S(1)} %bitcast.79, f32[2,3,48,96,96]{3,4,2,1,0:T(8,128)} %get-tuple-element.33, f32[2,3,48,96]{3,2,1,0:T(8,128)S(1)} %get-tuple-element.32), kind=kOutput, calls=%fused_computation.47 | convolution fusion | flops 176062464 | bytes 14266368 | tf_op jit(solution)/shard_map/bchqk,bqchd->bkchd/dot_general | solution.py:114
  296.5 4.0 copy.141
  300.4 34.6 %all_to_all.30 = bf16[2,96,3,1536]{3,0,2,1:T(2,128)(2,1)S(1)} all-to-all(bf16[2,96,3,1536]{3,0,2,1:T(2,128)(2,1)S(1)} %copy.141), channel_id=1, replica_groups=mesh['dp'=8,'grid'=32] {'grid'}, dimensions={1} | all-to-all | bytes 3538944 | tf_op jit(solution)/shard_map/all_to_all | solution.py:118
  339.2 7.1 %convolution_convert_fusion.1 = bf16[576,1536]{1,0:T(8,128)(2,1)} fusion(bf16[576,1536]{1,0:T(8,128)(2,1)} %reshape.135, bf16[1536,1536]{1,0:T(8,128)(2,1)} %reshape.140), kind=kOutput, calls=%fused_computation.41 | convolution fusion | flops 2718793728 | bytes 8257536 | tf_op jit(solution)/shard_map/dot_general | solution.py:120
  349.0 3.6 reshape.136
  352.6 11.7 %fusion = f32[6,48,96,96]{2,3,1,0:T(8,128)} fusion(bf16[6,96,48,32]{1,3,2,0:T(8,128)(2,1)} %bitcast.86, bf16[6,96,48,32]{1,0,3,2:T(8,128)(2,1)} %reshape.136, f32[6,48,96,96]{2,3,1,0:T(8,128)} %get-tuple-element.31, f32[6,48,96]{2,1,0:T(8,128)S(1)} %get-tuple-element.30), kind=kOutput, calls=%fused_computation | convolution fusion | flops 175205472 | bytes 24883200 | tf_op jit(solution)/shard_map/sub | solution.py:37
  364.3 13.7 %multiply_reduce_fusion = f32[48,96,96]{1,2,0:T(8,128)} fusion(f32[6,48,96,96]{2,3,1,0:T(8,128)} %fusion, f32[6,48,96,96]{2,3,1,0:T(8,128)} %get-tuple-element.31, f32[6,48,96]{2,1,0:T(8,128)S(1)} %get-tuple-element.30, bf16[6,96,48,32]{1,3,2,0:T(8,128)(2,1)} %bitcast.87, bf16[6,96,48,32]{1,0,3,2:T(8,128)(2,1)S(1)} %copy-done.2), kind=kOutput, calls=%fused_computation.8 | convolution fusion | flops 180043776 | bytes 26652672 | tf_op jit(solution)/shard_map/nqhd,nkhd->nhqk/dot_general | solution.py:124
  381.1 3.9 reshape.137
  385.0 5.3 %fusion.16 = f32[191,48]{0,1:T(8,128)S(1)} fusion(f32[9216,48]{0,1:T(8,128)} %reshape.137, s32[9216]{0:T(1024)S(1)} %copy-done.8), kind=kOutput, calls=%fused_computation.28 | convolution fusion | flops 1015667712 | bytes 1843008 | tf_op jit(solution)/shard_map/dot_general | solution.py:33
  390.3 106.0 %psum.15 = f32[191,48]{0,1:T(8,128)S(1)} all-reduce(f32[191,48]{0,1:T(8,128)S(1)} %fusion.16), channel_id=1, replica_groups=mesh['dp'=8,'grid'=32] {'dp','grid'}, use_global_device_ids=true, to_apply=%region_10.0 | all-reduce | flops 9168 | bytes 73344 | tf_op jit(solution)/shard_map/psum | solution.py:129
  496.3 8.5 %fusion.32 = bf16[2,3,48,32,96]{4,3,2,1,0:T(8,128)(2,1)} fusion(bf16[2,96,3,48,32]{1,4,3,2,0:T(8,128)(2,1)S(1)} %copy-done.1, f32[2,3,48,96,96]{3,4,2,1,0:T(8,128)} %get-tuple-element.33, f32[2,3,48,96]{3,2,1,0:T(8,128)S(1)} %get-tuple-element.32), kind=kOutput, calls=%fused_computation.46 | convolution fusion | flops 176062464 | bytes 14266368 | tf_op jit(solution)/shard_map/bchqk,bkchd->bqchd/dot_general | solution.py:102
  504.8 4.0 copy.146
  508.9 5.4 %reduce_sum.85 = f32[191,48]{0,1:T(8,128)S(1)} reduce(f32[256,191,48]{1,2,0:T(8,128)} %all-gather.8.cloned.1.call-done, f32[]{:T(128)} %constant.6.clone.1), dimensions={0}, to_apply=%region_7.0 | reduce | flops 2337840 | bytes 9424708 | tf_op jit(solution)/shard_map/reduce_sum | solution.py:112
  (58 shorter events, 43.6 us)
Async XLA Ops:
  7.2 2.3 copy-start
  7.2 166.5 %all-gather.6.cloned.1.call-start = ((), (), s32[]{:S(2)}) async-start(), calls=%async_computation.2 | async-start | bytes 6316032 | tf_op jit(solution)/shard_map/all_gather | solution.py:41
  8.8 120.6 %copy-start.7 = (s32[9216]{0:T(1024)}, s32[9216]{0:T(1024)S(1)}, u32[]{:S(2)}) copy-start(s32[9216]{0:T(1024)S(1)} %add.72) | copy-start | bytes 110596
  8.9 0.6 copy-start.12
  138.1 4.1 copy-start.5
  144.6 4.1 copy-start.3
  173.7 8.6 %copy-start.4 = (bf16[576,1536]{0,1:T(8,128)(2,1)S(1)}, bf16[576,1536]{0,1:T(8,128)(2,1)}, u32[]{:S(2)}) copy-start(bf16[576,1536]{0,1:T(8,128)(2,1)} %reshape.125) | copy-start | bytes 5308420
  190.6 4.9 copy-start.9
  190.6 34.1 %all-to-all-start = ((bf16[2,3,96,1536]{3,0,1,2:T(2,128)(2,1)}), bf16[2,3,96,1536]{3,0,1,2:T(2,128)(2,1)}, u32[]{:S(2)}, u32[]{:S(2)}) async-start(bf16[2,3,96,1536]{3,0,1,2:T(2,128)(2,1)} %copy.129), calls=%async_computation | async-start | bytes 3538944 | tf_op jit(solution)/shard_map/all_to_all | solution.py:90
  195.4 313.4 %all-gather.8.cloned.1.call-start = ((), (), s32[]{:S(2)}) async-start(), calls=%async_computation.3 | async-start | bytes 12632064 | tf_op jit(solution)/shard_map/all_gather | solution.py:112
  204.7 4.1 copy-start.6
  352.6 11.7 %copy-start.2 = (bf16[6,96,48,32]{1,0,3,2:T(8,128)(2,1)S(1)}, bf16[6,96,48,32]{1,0,3,2:T(8,128)(2,1)}, u32[]{:S(2)}) copy-start(bf16[6,96,48,32]{1,0,3,2:T(8,128)(2,1)} %reshape.136) | copy-start | bytes 5308420
  381.1 3.9 copy-start.8
  381.1 115.2 %copy-start.1 = (bf16[2,96,3,48,32]{1,4,3,2,0:T(8,128)(2,1)S(1)}, bf16[2,96,3,48,32]{1,4,3,2,0:T(8,128)(2,1)}, u32[]{:S(2)}) copy-start(bf16[2,96,3,48,32]{1,4,3,2,0:T(8,128)(2,1)} %copy.135) | copy-start | bytes 5308420
  508.8 5.4 %copy-start.10 = (f32[16]{0:T(128)S(1)}, f32[16]{0:T(128)}, u32[]{:S(2)}) copy-start(f32[16]{0:T(128)} %param.22) | copy-start | bytes 196
  508.8 5.4 %copy-start.11 = (f32[16]{0:T(128)S(1)}, f32[16]{0:T(128)}, u32[]{:S(2)}) copy-start(f32[16]{0:T(128)} %param.21) | copy-start | bytes 196
  508.8 5.4 %copy-start.13 = (f32[191]{0:T(256)S(1)}, f32[191]{0:T(256)}, u32[]{:S(2)}) copy-start(f32[191]{0:T(256)} %copy-done.12) | copy-start | bytes 2296
Sparse Core Ops, SparseCore 0:
  11.8 121.0 all-gather.5
  286.2 151.9 all-gather.7
